TPU v7x, 512 devices: a whole 4x8x8 slice. The times are simulated.
512 devices in a mesh: gz: 32 (over z_hi, x, core), gy: 16 (over z_lo, y).
Axes of the slice: x: 4, y: 8, z: 8 (z_hi: 4, z_lo: 2; z = z_hi * 2 + z_lo), core: 2. Of those that a mesh axis runs over, the one named last changes fastest.
Arguments:
- filtered: bfloat16 [16, 256, 4096], P(None, 'gz', 'gy'), may hold values from -6 to 6
- angle_index: int32 [16], replicated, may hold values from 0 to 3599
- band_offset: int32 [16, 32], P(None, 'gz'), may hold values from 0 to 12, as said below
- band_length: int32 [16, 32], P(None, 'gz'), may hold values from 4 to 12
- foot_block: int32 [16, 64, 64], P(None, 'gy'), may hold values from 0 to 62, as said below
Outputs:
- denoised: float32 [64, 256, 4096], P('gy', 'gz')
Inputs may be any that keep to these rules, and one draw needn't show every extreme that they name: band_offset + band_length <= 16 for every projection and group. foot_block[p, y, b] is b plus a shift of -2 to 2 that depends only on p and y, clipped to the range.
All inputs are finite; a program needn't handle non-finite values.
Results may differ from a plain program's by a relative error of at most 0.0041.
Values may be sent and summed in bfloat16 or wider, within the bound.
A program may use at most 64 MiB of HBM per device.

v0:
```python
import math
import jax
import jax.numpy as jnp
from jax import lax
from jax.sharding import PartitionSpec as P

X = 4096
P_SIZE = 16
NANG = 3600
BLOCK = 64
ITERS = 2
step_length = 0.25
smooth_weight = 0.3
gradient_floor = 0.01
shift_reach = 8.0


def with_halo(cells, sides, width):
    for axis, dim in sides:
        count = lax.axis_size(axis)
        ends = count - 1
        head = lax.slice_in_dim(cells, 0, width, axis=dim)
        tail = lax.slice_in_dim(cells, cells.shape[dim] - width, cells.shape[dim], axis=dim)
        cells = jnp.concatenate(
            [
                lax.ppermute(tail, axis, [(i, (i + 1) % count) for i in range(ends)]),
                cells,
                lax.ppermute(head, axis, [((i + 1) % count, i) for i in range(ends)]),
            ],
            axis=dim,
        )
    return cells


def geometry(angle_value):
    radians = 2.0 * math.pi * angle_value.astype(jnp.float32) / NANG
    stretch = 0.5 + 0.5 * jnp.abs(jnp.cos(radians))
    spread = 1.0 + jnp.abs(jnp.sin(radians))
    return (radians, stretch, spread)


def footprint(radians, stretch, spread, row_global, rows_total, block_size):
    shifted = shift_reach * jnp.sin(radians + 2.0 * math.pi * row_global / rows_total)
    inside = jnp.arange(block_size).astype(jnp.float32) - 0.5 * (block_size - 1)
    centre = block_size + inside[None, :] * stretch + shifted[:, None]
    places = jnp.arange(2 * block_size).astype(jnp.float32) + 0.5
    weights = (
        jnp.maximum(0.0, 1.0 - jnp.abs(places[None, None, :] - centre[:, :, None]) / spread)
        / spread
    )
    return weights.astype(jnp.bfloat16)


def axial_table(offsets, lengths, depth_count):
    offset_real = offsets.astype(jnp.float32)[..., None]
    length_real = lengths.astype(jnp.float32)[..., None]
    depth_place = jnp.arange(depth_count).astype(jnp.float32) + 0.5
    centre = offset_real + depth_place * length_real / depth_count
    row_number = jnp.arange(2 * depth_count)
    row_place = row_number.astype(jnp.float32) + 0.5
    triangle = jnp.maximum(0.0, 1.0 - jnp.abs(row_place - centre[..., None]))
    inside = (row_number >= offsets[..., None, None]) & (
        row_number < (offsets + lengths)[..., None, None]
    )
    return jnp.where(inside, triangle, 0.0).astype(jnp.bfloat16)


def smooth_update(current, fidelity, row_first, depth_first, rows_total, depth_total):
    row_index = row_first + jnp.arange(current.shape[0])
    depth_index = depth_first + jnp.arange(current.shape[1])
    keep_rows = ((row_index >= 0) & (row_index < rows_total - 1)).astype(jnp.float32)[:, None, None]
    keep_depth = ((depth_index >= 0) & (depth_index < depth_total - 1)).astype(jnp.float32)[
        None, :, None
    ]
    forward_rows = (
        jnp.concatenate([current[1:] - current[:-1], jnp.zeros_like(current[:1])], 0) * keep_rows
    )
    forward_depth = (
        jnp.concatenate([current[:, 1:] - current[:, :-1], jnp.zeros_like(current[:, :1])], 1)
        * keep_depth
    )
    forward_width = jnp.concatenate(
        [current[:, :, 1:] - current[:, :, :-1], jnp.zeros_like(current[:, :, :1])], 2
    )
    magnitude = jnp.sqrt(
        forward_rows * forward_rows
        + forward_depth * forward_depth
        + forward_width * forward_width
        + gradient_floor
    )
    normal_rows = forward_rows / magnitude
    normal_depth = forward_depth / magnitude
    normal_width = forward_width / magnitude
    divergence = normal_rows - jnp.concatenate(
        [jnp.zeros_like(normal_rows[:1]), normal_rows[:-1]], 0
    )
    divergence = (
        divergence
        + normal_depth
        - jnp.concatenate([jnp.zeros_like(normal_depth[:, :1]), normal_depth[:, :-1]], 1)
    )
    divergence = (
        divergence
        + normal_width
        - jnp.concatenate([jnp.zeros_like(normal_width[:, :, :1]), normal_width[:, :, :-1]], 2)
    )
    return current + step_length * (smooth_weight * divergence - (current - fidelity))


def per_device(filtered, angle_index, band_offset, band_length, foot_block):
    depth_count = filtered.shape[1]
    row_count = foot_block.shape[1]
    extended_band = with_halo(filtered, (("gz", 1),), depth_count // 2)
    axial_weights = axial_table(band_offset[:, 0], band_length[:, 0], depth_count)
    summed_rows = jnp.einsum(
        "pzv,pvu->pzu", axial_weights, extended_band, preferred_element_type=jnp.float32
    )
    columns = lax.all_gather(summed_rows.astype(jnp.bfloat16), "gy", axis=2, tiled=True)
    column_count = columns.shape[2]
    row_base = lax.axis_index("gy") * row_count
    depth_base = lax.axis_index("gz") * depth_count
    rows_total = lax.axis_size("gy") * row_count
    depth_total = lax.axis_size("gz") * depth_count
    row_global = (row_base + jnp.arange(row_count)).astype(jnp.float32)

    def one_projection(running, inputs):
        projected, angle_value, blocks = inputs
        radians, stretch, spread = geometry(angle_value)
        weights = footprint(radians, stretch, spread, row_global, rows_total, BLOCK)
        column_tiles = projected.reshape(depth_count, column_count // BLOCK, BLOCK)
        window = jnp.concatenate([column_tiles[:, blocks], column_tiles[:, blocks + 1]], axis=-1)
        product = jnp.einsum("yiu,zybu->yzbi", weights, window, preferred_element_type=jnp.float32)
        return (running + product.reshape(running.shape), None)

    initial = jnp.zeros((row_count, depth_count, X), jnp.float32)
    summed, _unused = lax.scan(one_projection, initial, (columns, angle_index, foot_block))
    backprojection = math.pi / P_SIZE * summed
    current = backprojection
    padded_fidelity = jnp.pad(backprojection, ((1, 1), (1, 1), (0, 0)))
    for turn_index in range(ITERS):
        extended = with_halo(current, (("gz", 1), ("gy", 0)), 1)
        updated = smooth_update(
            extended, padded_fidelity, row_base - 1, depth_base - 1, rows_total, depth_total
        )
        current = updated[1:-1, 1:-1]
    return current


def solution(mesh):
    return jax.shard_map(
        per_device,
        mesh=mesh,
        in_specs=(P(None, "gz", "gy"), P(), P(None, "gz"), P(None, "gz"), P(None, "gy", None)),
        out_specs=P("gy", "gz", None),
        check_vma=False,
    )
```

profile of v0, /device:TPU:191, one launch (start us, length us, event | category | flops | bytes accessed | tf_op | source)
XLA Modules:
  0.0 272.2 jit_solution(10231032295771682402)
XLA Ops:
  6.5 0.9 fusion.43
  7.5 7.5 %collective-permute-start = (bf16[16,4,256]{2,1,0:T(4,128)(2,1)S(1)}, bf16[16,4,256]{2,1,0:T(4,128)(2,1)S(1)}, u32[]{:S(2)}, u32[]{:S(2)}) collective-permute-start(bf16[16,4,256]{2,1,0:T(4,128)(2,1)S(1)} %get-tuple-element.140), channel_id=1, source_target_pairs={{0,16},{16,32},{32,48},{48,64},{64,80},{80,96},{96,112},{112,128},... | collective-permute-start | bytes 98312 | tf_op jit(solution)/shard_map/ppermute | solution.py:26
  15.0 1.9 collective-permute-start.1
  19.1 5.4 %collective-permute-done.1 = bf16[16,4,256]{2,1,0:T(4,128)(2,1)S(1)} collective-permute-done((bf16[16,4,256]{2,1,0:T(4,128)(2,1)S(1)}, bf16[16,4,256]{2,1,0:T(4,128)(2,1)S(1)}, u32[]{:S(2)}, u32[]{:S(2)}) %collective-permute-start.1) | collective-permute-done | bytes 32800 | tf_op jit(solution)/shard_map/ppermute | solution.py:28
  24.4 1.7 convolution_convert_fusion
  26.2 55.3 %all-gather.2.cloned.1.call-done = bf16[16,8,4096]{2,1,0:T(8,128)(2,1)} async-done(((bf16[16,8,256]{2,1,0:T(8,128)(2,1)}), bf16[16,8,4096]{2,1,0:T(8,128)(2,1)}) %all-gather.2.cloned.1.call-update) | async-done | bytes 1048592 | tf_op jit(solution)/shard_map/all_gather | solution.py:118
  81.4 113.9 %while.13 = (s32[]{:T(128)}, f32[4,8,4096]{2,1,0:T(8,128)S(1)}, bf16[16,8,4096]{2,1,0:T(8,128)(2,1)}, s32[16,4,64]{2,1,0:T(4,128)}, s32[16]{0:T(128)}, /*index=5...) while((s32[]{:T(128)}, f32[4,8,4096]{2,1,0:T(8,128)S(1)}, ...), condition=%wide.region_1.2_spmd.clone, body=%wide.region_0.1_spmd.clone.sunk | while | flops 35099164 | bytes 6183707 | solution.py:136
  81.4 1.2 dynamic_slice.32
  84.5 0.9 constant_dynamic-slice_fusion.2
  88.6 1.2 dynamic_slice.32
  95.7 1.2 dynamic_slice.32
  98.7 0.9 constant_dynamic-slice_fusion.2
  102.8 1.2 dynamic_slice.32
  105.9 0.9 constant_dynamic-slice_fusion.2
  109.9 1.2 dynamic_slice.32
  113.0 0.9 constant_dynamic-slice_fusion.2
  117.0 1.2 dynamic_slice.32
  124.2 1.2 dynamic_slice.32
  127.2 0.9 constant_dynamic-slice_fusion.2
  131.3 1.2 dynamic_slice.32
  138.4 1.2 dynamic_slice.32
  145.5 1.2 dynamic_slice.32
  148.6 0.9 constant_dynamic-slice_fusion.2
  152.6 1.2 dynamic_slice.32
  159.8 1.2 dynamic_slice.32
  166.9 1.2 dynamic_slice.32
  174.0 1.2 dynamic_slice.32
  181.1 1.2 dynamic_slice.32
  188.2 1.2 dynamic_slice.32
  191.3 0.9 constant_dynamic-slice_fusion.2
  195.5 15.9 %collective-permute-start.2 = (f32[4,1,4096]{2,1,0:T(1,128)S(1)}, f32[4,1,4096]{2,1,0:T(1,128)S(1)}, u32[]{:S(2)}, u32[]{:S(2)}) collective-permute-start(f32[4,1,4096]{2,1,0:T(1,128)S(1)} %get-tuple-element.138), channel_id=1, source_target_pairs={{0,16},{16,32},{32,48},{48,64},{64,80},{80,96},{96,112},{112,128},... | collective-permute-start | bytes 196616 | tf_op jit(solution)/shard_map/ppermute | solution.py:26
  211.4 1.9 collective-permute-start.3
  213.3 7.9 %collective-permute-done.3 = f32[4,1,4096]{2,1,0:T(1,128)S(1)} collective-permute-done((f32[4,1,4096]{2,1,0:T(1,128)S(1)}, f32[4,1,4096]{2,1,0:T(1,128)S(1)}, u32[]{:S(2)}, u32[]{:S(2)}) %collective-permute-start.3) | collective-permute-done | bytes 65568 | tf_op jit(solution)/shard_map/ppermute | solution.py:28
  221.3 2.9 %collective-permute-start.4 = (f32[1,10,4096]{2,1,0:T(8,128)S(1)}, f32[1,10,4096]{2,1,0:T(8,128)S(1)}, u32[]{:S(2)}, u32[]{:S(2)}) collective-permute-start(f32[1,10,4096]{2,1,0:T(8,128)S(1)} %get-tuple-element.136), channel_id=1, source_target_pairs={{0,1},{1,2},{2,3},{3,4},{4,5},{5,6},{6,7},{7,8},{8,9},{9,10},{10,1... | collective-permute-start | bytes 491528 | tf_op jit(solution)/shard_map/ppermute | solution.py:26
  224.2 2.3 collective-permute-start.5
  226.6 1.8 collective-permute-done.4
  228.4 5.1 %collective-permute-done.5 = f32[1,10,4096]{2,1,0:T(8,128)S(1)} collective-permute-done((f32[1,10,4096]{2,1,0:T(8,128)S(1)}, f32[1,10,4096]{2,1,0:T(8,128)S(1)}, u32[]{:S(2)}, u32[]{:S(2)}) %collective-permute-start.5) | collective-permute-done | bytes 163872 | tf_op jit(solution)/shard_map/ppermute | solution.py:28
  234.6 1.1 fusion.19
  235.8 1.2 multiply_add_fusion.1
  237.1 3.3 %collective-permute-start.6 = (f32[4,1,4096]{2,1,0:T(1,128)S(1)}, f32[4,1,4096]{2,1,0:T(1,128)S(1)}, u32[]{:S(2)}, u32[]{:S(2)}) collective-permute-start(f32[4,1,4096]{2,1,0:T(1,128)S(1)} %get-tuple-element.132), channel_id=1, source_target_pairs={{0,16},{16,32},{32,48},{48,64},{64,80},{80,96},{96,112},{112,128},... | collective-permute-start | bytes 196616 | tf_op jit(solution)/shard_map/ppermute | solution.py:26
  240.4 1.9 collective-permute-start.7
  242.4 7.8 %collective-permute-done.7 = f32[4,1,4096]{2,1,0:T(1,128)S(1)} collective-permute-done((f32[4,1,4096]{2,1,0:T(1,128)S(1)}, f32[4,1,4096]{2,1,0:T(1,128)S(1)}, u32[]{:S(2)}, u32[]{:S(2)}) %collective-permute-start.7) | collective-permute-done | bytes 65568 | tf_op jit(solution)/shard_map/ppermute | solution.py:28
  250.3 1.9 collective-permute-start.8
  252.2 3.4 %collective-permute-start.9 = (f32[1,10,4096]{2,1,0:T(8,128)S(1)}, f32[1,10,4096]{2,1,0:T(8,128)S(1)}, u32[]{:S(2)}, u32[]{:S(2)}) collective-permute-start(f32[1,10,4096]{2,1,0:T(8,128)S(1)} %get-tuple-element.135), channel_id=1, source_target_pairs={{1,0},{2,1},{3,2},{4,3},{5,4},{6,5},{7,6},{8,7},{9,8},{10,9},{11,1... | collective-permute-start | bytes 491528 | tf_op jit(solution)/shard_map/ppermute | solution.py:28
  255.6 1.8 collective-permute-done.8
  257.4 4.0 %collective-permute-done.9 = f32[1,10,4096]{2,1,0:T(8,128)S(1)} collective-permute-done((f32[1,10,4096]{2,1,0:T(8,128)S(1)}, f32[1,10,4096]{2,1,0:T(8,128)S(1)}, u32[]{:S(2)}, u32[]{:S(2)}) %collective-permute-start.9) | collective-permute-done | bytes 163872 | tf_op jit(solution)/shard_map/ppermute | solution.py:28
  262.5 1.1 fusion.20
  264.2 1.2 fusion.25
  (312 shorter events, 79.3 us)
Async XLA Ops:
  6.5 74.9 %all-gather.2.cloned.1.call-start = ((), (), s32[]{:S(2)}) async-start(), calls=%async_computation | async-start | bytes 1114112 | tf_op jit(solution)/shard_map/all_gather | solution.py:118
  7.5 11.6 %collective-permute-start = (bf16[16,4,256]{2,1,0:T(4,128)(2,1)S(1)}, bf16[16,4,256]{2,1,0:T(4,128)(2,1)S(1)}, u32[]{:S(2)}, u32[]{:S(2)}) collective-permute-start(bf16[16,4,256]{2,1,0:T(4,128)(2,1)S(1)} %get-tuple-element.140), channel_id=1, source_target_pairs={{0,16},{16,32},{32,48},{48,64},{64,80},{80,96},{96,112},{112,128},... | collective-permute-start | bytes 98312 | tf_op jit(solution)/shard_map/ppermute | solution.py:26
  15.0 9.5 %collective-permute-start.1 = (bf16[16,4,256]{2,1,0:T(4,128)(2,1)S(1)}, bf16[16,4,256]{2,1,0:T(4,128)(2,1)S(1)}, u32[]{:S(2)}, u32[]{:S(2)}) collective-permute-start(bf16[16,4,256]{2,1,0:T(4,128)(2,1)S(1)} %get-tuple-element.141), channel_id=1, source_target_pairs={{16,0},{32,16},{48,32},{64,48},{80,64},{96,80},{112,96},{128,112},... | collective-permute-start | bytes 98312 | tf_op jit(solution)/shard_map/ppermute | solution.py:28
  195.5 17.8 %collective-permute-start.2 = (f32[4,1,4096]{2,1,0:T(1,128)S(1)}, f32[4,1,4096]{2,1,0:T(1,128)S(1)}, u32[]{:S(2)}, u32[]{:S(2)}) collective-permute-start(f32[4,1,4096]{2,1,0:T(1,128)S(1)} %get-tuple-element.138), channel_id=1, source_target_pairs={{0,16},{16,32},{32,48},{48,64},{64,80},{80,96},{96,112},{112,128},... | collective-permute-start | bytes 196616 | tf_op jit(solution)/shard_map/ppermute | solution.py:26
  211.4 9.8 %collective-permute-start.3 = (f32[4,1,4096]{2,1,0:T(1,128)S(1)}, f32[4,1,4096]{2,1,0:T(1,128)S(1)}, u32[]{:S(2)}, u32[]{:S(2)}) collective-permute-start(f32[4,1,4096]{2,1,0:T(1,128)S(1)} %get-tuple-element.139), channel_id=1, source_target_pairs={{16,0},{32,16},{48,32},{64,48},{80,64},{96,80},{112,96},{128,112},... | collective-permute-start | bytes 196616 | tf_op jit(solution)/shard_map/ppermute | solution.py:28
  221.3 7.1 %collective-permute-start.4 = (f32[1,10,4096]{2,1,0:T(8,128)S(1)}, f32[1,10,4096]{2,1,0:T(8,128)S(1)}, u32[]{:S(2)}, u32[]{:S(2)}) collective-permute-start(f32[1,10,4096]{2,1,0:T(8,128)S(1)} %get-tuple-element.136), channel_id=1, source_target_pairs={{0,1},{1,2},{2,3},{3,4},{4,5},{5,6},{6,7},{7,8},{8,9},{9,10},{10,1... | collective-permute-start | bytes 491528 | tf_op jit(solution)/shard_map/ppermute | solution.py:26
  224.2 9.2 %collective-permute-start.5 = (f32[1,10,4096]{2,1,0:T(8,128)S(1)}, f32[1,10,4096]{2,1,0:T(8,128)S(1)}, u32[]{:S(2)}, u32[]{:S(2)}) collective-permute-start(f32[1,10,4096]{2,1,0:T(8,128)S(1)} %get-tuple-element.137), channel_id=1, source_target_pairs={{1,0},{2,1},{3,2},{4,3},{5,4},{6,5},{7,6},{8,7},{9,8},{10,9},{11,1... | collective-permute-start | bytes 491528 | tf_op jit(solution)/shard_map/ppermute | solution.py:28
  237.1 5.3 %collective-permute-start.6 = (f32[4,1,4096]{2,1,0:T(1,128)S(1)}, f32[4,1,4096]{2,1,0:T(1,128)S(1)}, u32[]{:S(2)}, u32[]{:S(2)}) collective-permute-start(f32[4,1,4096]{2,1,0:T(1,128)S(1)} %get-tuple-element.132), channel_id=1, source_target_pairs={{0,16},{16,32},{32,48},{48,64},{64,80},{80,96},{96,112},{112,128},... | collective-permute-start | bytes 196616 | tf_op jit(solution)/shard_map/ppermute | solution.py:26
  240.4 9.8 %collective-permute-start.7 = (f32[4,1,4096]{2,1,0:T(1,128)S(1)}, f32[4,1,4096]{2,1,0:T(1,128)S(1)}, u32[]{:S(2)}, u32[]{:S(2)}) collective-permute-start(f32[4,1,4096]{2,1,0:T(1,128)S(1)} %get-tuple-element.133), channel_id=1, source_target_pairs={{16,0},{32,16},{48,32},{64,48},{80,64},{96,80},{112,96},{128,112},... | collective-permute-start | bytes 196616 | tf_op jit(solution)/shard_map/ppermute | solution.py:28
  250.3 7.1 %collective-permute-start.8 = (f32[1,10,4096]{2,1,0:T(8,128)S(1)}, f32[1,10,4096]{2,1,0:T(8,128)S(1)}, u32[]{:S(2)}, u32[]{:S(2)}) collective-permute-start(f32[1,10,4096]{2,1,0:T(8,128)S(1)} %get-tuple-element.134), channel_id=1, source_target_pairs={{0,1},{1,2},{2,3},{3,4},{4,5},{5,6},{6,7},{7,8},{8,9},{9,10},{10,1... | collective-permute-start | bytes 491528 | tf_op jit(solution)/shard_map/ppermute | solution.py:26
  252.2 9.2 %collective-permute-start.9 = (f32[1,10,4096]{2,1,0:T(8,128)S(1)}, f32[1,10,4096]{2,1,0:T(8,128)S(1)}, u32[]{:S(2)}, u32[]{:S(2)}) collective-permute-start(f32[1,10,4096]{2,1,0:T(8,128)S(1)} %get-tuple-element.135), channel_id=1, source_target_pairs={{1,0},{2,1},{3,2},{4,3},{5,4},{6,5},{7,6},{8,7},{9,8},{10,9},{11,1... | collective-permute-start | bytes 491528 | tf_op jit(solution)/shard_map/ppermute | solution.py:28
Sparse Core Ops, SparseCore 0:
  26.3 55.1 all-gather.1
where the time goes:
time: 274 us; the launch traced here: 272 us
  waiting for transfers between devices  89 us (32%)
  local copies, waits for them, and re-layouts  77.9 us (28%)
  starting transfers between devices  43 us (16%)
  other arithmetic  25.3 us (9%)
  loops' own time  14.1 us (5%)
  between operations  13.7 us (5%)
  matrix products  9.14 us (3%)
    all_gather x1, waiting for transfers between devices, per_device(): lax.all_gather(summed_rows.astype(jnp.bfloat16), 'gy', axis=2, tiled=True)  55.3 us
    dynamic_slice x32, local copies, waits for them, and re-layouts, per_device(): lax.scan(one_projection, initial, (columns, angle_index, foot_block))  33.5 us
    ppermute x5, starting transfers between devices, with_halo(): lax.ppermute(tail, axis, [(i, (i + 1) % count) for i in range(ends)])  31.5 us
    ppermute x5, waiting for transfers between devices, with_halo(): lax.ppermute(head, axis, [((i + 1) % count, i) for i in range(ends)])  30.1 us
    gather x32, local copies, waits for them, and re-layouts, one_projection(): column_tiles[:, blocks + 1]  17.4 us
    another operation x1, loops' own time, per_device(): lax.scan(one_projection, initial, (columns, angle_index, foot_block))  14.1 us
    gather x16, local copies, waits for them, and re-layouts, one_projection(): column_tiles[:, blocks]  13.1 us
    ppermute x5, starting transfers between devices, with_halo(): lax.ppermute(head, axis, [((i + 1) % count, i) for i in range(ends)])  11.5 us
  transfers between devices with their start and end apart: 11, of which 8 were waited for; matrix products, arithmetic and copies ran while one was open for 1% of the time, Pallas kernels for 0%

commit v1 on v0

--- a/solution.py
+++ b/solution.py
@@ -115,7 +115,12 @@
     summed_rows = jnp.einsum(
         "pzv,pvu->pzu", axial_weights, extended_band, preferred_element_type=jnp.float32
     )
-    columns = lax.all_gather(summed_rows.astype(jnp.bfloat16), "gy", axis=2, tiled=True)
+    columns = jnp.concatenate(
+        lax.all_to_all(
+            jnp.stack([summed_rows.astype(jnp.bfloat16)] * lax.axis_size("gy")), "gy", 0, 0
+        ),
+        axis=2,
+    )
     column_count = columns.shape[2]
     row_base = lax.axis_index("gy") * row_count
     depth_base = lax.axis_index("gz") * depth_count

time: 274 us -> 200 us (0.73)
  waiting for transfers between devices: 89 us -> 54.4 us
  local copies, waits for them, and re-layouts: 77.9 us -> 56.3 us
  between operations: 13.7 us -> 0.31 us
  starting transfers between devices: 43 us -> 39.7 us
    all_gather x1 -> x0, waiting for transfers between devices: 55.3 us -> none  [per_device(): lax.all_gather(summed_rows.astype(jnp.bfloat16), 'gy', axis=2, tiled=True)]
    dynamic_slice x32, local copies, waits for them, and re-layouts: 33.5 us -> 10.6 us  [per_device(): lax.scan(one_projection, initial, (columns, angle_index, foot_block))]
    all_to_all x0 -> x1, waiting for transfers between devices: none -> 20.4 us  [per_device(): lax.all_to_all(jnp.stack([summed_rows.astype(jnp.bfloat16)] * lax.axis_si...]
    ppermute x5, starting transfers between devices: 31.5 us -> 21.2 us  [with_halo(): lax.ppermute(tail, axis, [(i, (i + 1) % count) for i in range(ends)])]
    all_to_all x0 -> x1, starting transfers between devices: none -> 7.28 us  [per_device(): lax.all_to_all(jnp.stack([summed_rows.astype(jnp.bfloat16)] * lax.axis_si...]
where the time goes in v1:
time: 200 us; the launch traced here: 199 us
  local copies, waits for them, and re-layouts  56.3 us (28%)
  waiting for transfers between devices  54.4 us (27%)
  starting transfers between devices  39.7 us (20%)
  other arithmetic  25.4 us (13%)
  loops' own time  13.9 us (7%)
  matrix products  8.51 us (4%)
    ppermute x5, waiting for transfers between devices, with_halo(): lax.ppermute(head, axis, [((i + 1) % count, i) for i in range(ends)])  30.3 us
    ppermute x5, starting transfers between devices, with_halo(): lax.ppermute(tail, axis, [(i, (i + 1) % count) for i in range(ends)])  21.2 us
    all_to_all x1, waiting for transfers between devices, per_device(): lax.all_to_all(jnp.stack([summed_rows.astype(jnp.bfloat16)] * lax.axis_si...  20.4 us
    gather x32, local copies, waits for them, and re-layouts, one_projection(): column_tiles[:, blocks + 1]  17.4 us
    another operation x1, loops' own time, per_device(): lax.scan(one_projection, initial, (columns, angle_index, foot_block))  13.9 us
    gather x16, local copies, waits for them, and re-layouts, one_projection(): column_tiles[:, blocks]  13.1 us
    ppermute x5, starting transfers between devices, with_halo(): lax.ppermute(head, axis, [((i + 1) % count, i) for i in range(ends)])  11.3 us
    select_n x16, other arithmetic, one_projection(): column_tiles[:, blocks]  11 us
  transfers between devices with their start and end apart: 11, of which 8 were waited for; matrix products, arithmetic and copies ran while one was open for 1% of the time, Pallas kernels for 0%

profile of v1, /device:TPU:191, one launch (start us, length us, event | category | flops | bytes accessed | tf_op | source)
XLA Modules:
  0.0 198.5 jit_solution(4540691804645319273)
XLA Ops:
  0.0 0.9 fusion.43
  0.9 7.5 %collective-permute-start = (bf16[16,4,256]{2,1,0:T(4,128)(2,1)S(1)}, bf16[16,4,256]{2,1,0:T(4,128)(2,1)S(1)}, u32[]{:S(2)}, u32[]{:S(2)}) collective-permute-start(bf16[16,4,256]{2,1,0:T(4,128)(2,1)S(1)} %get-tuple-element.140), channel_id=1, source_target_pairs={{0,16},{16,32},{32,48},{48,64},{64,80},{80,96},{96,112},{112,128},... | collective-permute-start | bytes 98312 | tf_op jit(solution)/shard_map/ppermute | solution.py:26
  8.4 1.9 collective-permute-start.1
  12.6 5.4 %collective-permute-done.1 = bf16[16,4,256]{2,1,0:T(4,128)(2,1)S(1)} collective-permute-done((bf16[16,4,256]{2,1,0:T(4,128)(2,1)S(1)}, bf16[16,4,256]{2,1,0:T(4,128)(2,1)S(1)}, u32[]{:S(2)}, u32[]{:S(2)}) %collective-permute-start.1) | collective-permute-done | bytes 32800 | tf_op jit(solution)/shard_map/ppermute | solution.py:28
  17.9 1.0 convolution_convert_fusion
  19.0 1.1 stack.2
  20.1 7.3 %all-to-all-start = ((bf16[16,16,8,256]{3,2,1,0:T(8,128)(2,1)}), bf16[16,16,8,256]{3,2,1,0:T(8,128)(2,1)S(1)}, u32[]{:S(2)}, u32[]{:S(2)}) async-start(bf16[16,16,8,256]{3,2,1,0:T(8,128)(2,1)} %stack.2), calls=%async_computation | async-start | bytes 2097152 | tf_op jit(solution)/shard_map/all_to_all | solution.py:119
  27.4 20.4 %all-to-all-done = bf16[16,16,8,256]{3,2,1,0:T(8,128)(2,1)S(1)} async-done(((bf16[16,16,8,256]{3,2,1,0:T(8,128)(2,1)}), bf16[16,16,8,256]{3,2,1,0:T(8,128)(2,1)S(1)}, u32[]{:S(2)}, u32[]{:S(2)}) %all-to-all-start) | async-done | bytes 1048608 | tf_op jit(solution)/shard_map/all_to_all | solution.py:119
  47.9 90.8 %while.13 = (s32[]{:T(128)}, f32[4,8,4096]{2,1,0:T(8,128)S(1)}, bf16[16,8,4096]{2,1,0:T(8,128)(2,1)S(1)}, s32[16,4,64]{2,1,0:T(4,128)}, s32[16]{0:T(128)S(1)}, /...) while((s32[]{:T(128)}, f32[4,8,4096]{2,1,0:T(8,128)S(1)}, ...), condition=%wide.region_1.2_spmd.clone, body=%wide.region_0.1_spmd.clone.sunk | while | flops 35099164 | bytes 6183707 | solution.py:141
  51.5 0.8 gather_fusion
  56.3 0.8 gather_fusion.1
  57.2 0.8 gather_fusion
  62.8 0.8 gather_fusion
  67.7 0.8 gather_fusion.1
  73.4 0.8 gather_fusion.1
  74.2 0.8 gather_fusion
  79.1 0.8 gather_fusion.1
  84.7 0.8 gather_fusion.1
  90.4 0.8 gather_fusion.1
  91.2 0.8 gather_fusion
  96.1 0.8 gather_fusion.1
  96.9 0.8 gather_fusion
  101.8 0.8 gather_fusion.1
  102.6 0.8 gather_fusion
  108.3 0.8 gather_fusion
  113.1 0.8 gather_fusion.1
  119.6 0.8 gather_fusion
  124.5 0.8 gather_fusion.1
  130.1 0.8 gather_fusion.1
  135.8 0.8 gather_fusion.1
  138.9 5.4 %collective-permute-start.2 = (f32[4,1,4096]{2,1,0:T(1,128)S(1)}, f32[4,1,4096]{2,1,0:T(1,128)S(1)}, u32[]{:S(2)}, u32[]{:S(2)}) collective-permute-start(f32[4,1,4096]{2,1,0:T(1,128)S(1)} %get-tuple-element.138), channel_id=1, source_target_pairs={{0,16},{16,32},{32,48},{48,64},{64,80},{80,96},{96,112},{112,128},... | collective-permute-start | bytes 196616 | tf_op jit(solution)/shard_map/ppermute | solution.py:26
  144.3 1.9 collective-permute-start.3
  146.2 7.9 %collective-permute-done.3 = f32[4,1,4096]{2,1,0:T(1,128)S(1)} collective-permute-done((f32[4,1,4096]{2,1,0:T(1,128)S(1)}, f32[4,1,4096]{2,1,0:T(1,128)S(1)}, u32[]{:S(2)}, u32[]{:S(2)}) %collective-permute-start.3) | collective-permute-done | bytes 65568 | tf_op jit(solution)/shard_map/ppermute | solution.py:28
  154.2 2.7 %collective-permute-start.4 = (f32[1,10,4096]{2,1,0:T(8,128)S(1)}, f32[1,10,4096]{2,1,0:T(8,128)S(1)}, u32[]{:S(2)}, u32[]{:S(2)}) collective-permute-start(f32[1,10,4096]{2,1,0:T(8,128)S(1)} %get-tuple-element.136), channel_id=1, source_target_pairs={{0,1},{1,2},{2,3},{3,4},{4,5},{5,6},{6,7},{7,8},{8,9},{9,10},{10,1... | collective-permute-start | bytes 491528 | tf_op jit(solution)/shard_map/ppermute | solution.py:26
  156.9 2.6 %collective-permute-start.5 = (f32[1,10,4096]{2,1,0:T(8,128)S(1)}, f32[1,10,4096]{2,1,0:T(8,128)S(1)}, u32[]{:S(2)}, u32[]{:S(2)}) collective-permute-start(f32[1,10,4096]{2,1,0:T(8,128)S(1)} %get-tuple-element.137), channel_id=1, source_target_pairs={{1,0},{2,1},{3,2},{4,3},{5,4},{6,5},{7,6},{8,7},{9,8},{10,9},{11,1... | collective-permute-start | bytes 491528 | tf_op jit(solution)/shard_map/ppermute | solution.py:28
  159.5 1.8 collective-permute-done.4
  161.3 4.8 %collective-permute-done.5 = f32[1,10,4096]{2,1,0:T(8,128)S(1)} collective-permute-done((f32[1,10,4096]{2,1,0:T(8,128)S(1)}, f32[1,10,4096]{2,1,0:T(8,128)S(1)}, u32[]{:S(2)}, u32[]{:S(2)}) %collective-permute-start.5) | collective-permute-done | bytes 163872 | tf_op jit(solution)/shard_map/ppermute | solution.py:28
  167.2 1.1 fusion.19
  168.4 1.2 multiply_add_fusion.1
  169.7 3.3 %collective-permute-start.6 = (f32[4,1,4096]{2,1,0:T(1,128)S(1)}, f32[4,1,4096]{2,1,0:T(1,128)S(1)}, u32[]{:S(2)}, u32[]{:S(2)}) collective-permute-start(f32[4,1,4096]{2,1,0:T(1,128)S(1)} %get-tuple-element.132), channel_id=1, source_target_pairs={{0,16},{16,32},{32,48},{48,64},{64,80},{80,96},{96,112},{112,128},... | collective-permute-start | bytes 196616 | tf_op jit(solution)/shard_map/ppermute | solution.py:26
  173.0 1.9 collective-permute-start.7
  175.0 7.8 %collective-permute-done.7 = f32[4,1,4096]{2,1,0:T(1,128)S(1)} collective-permute-done((f32[4,1,4096]{2,1,0:T(1,128)S(1)}, f32[4,1,4096]{2,1,0:T(1,128)S(1)}, u32[]{:S(2)}, u32[]{:S(2)}) %collective-permute-start.7) | collective-permute-done | bytes 65568 | tf_op jit(solution)/shard_map/ppermute | solution.py:28
  182.9 2.4 %collective-permute-start.8 = (f32[1,10,4096]{2,1,0:T(8,128)S(1)}, f32[1,10,4096]{2,1,0:T(8,128)S(1)}, u32[]{:S(2)}, u32[]{:S(2)}) collective-permute-start(f32[1,10,4096]{2,1,0:T(8,128)S(1)} %get-tuple-element.134), channel_id=1, source_target_pairs={{0,1},{1,2},{2,3},{3,4},{4,5},{5,6},{6,7},{7,8},{8,9},{9,10},{10,1... | collective-permute-start | bytes 491528 | tf_op jit(solution)/shard_map/ppermute | solution.py:26
  185.3 2.9 %collective-permute-start.9 = (f32[1,10,4096]{2,1,0:T(8,128)S(1)}, f32[1,10,4096]{2,1,0:T(8,128)S(1)}, u32[]{:S(2)}, u32[]{:S(2)}) collective-permute-start(f32[1,10,4096]{2,1,0:T(8,128)S(1)} %get-tuple-element.135), channel_id=1, source_target_pairs={{1,0},{2,1},{3,2},{4,3},{5,4},{6,5},{7,6},{8,7},{9,8},{10,9},{11,1... | collective-permute-start | bytes 491528 | tf_op jit(solution)/shard_map/ppermute | solution.py:28
  188.2 1.8 collective-permute-done.8
  190.0 4.5 %collective-permute-done.9 = f32[1,10,4096]{2,1,0:T(8,128)S(1)} collective-permute-done((f32[1,10,4096]{2,1,0:T(8,128)S(1)}, f32[1,10,4096]{2,1,0:T(8,128)S(1)}, u32[]{:S(2)}, u32[]{:S(2)}) %collective-permute-start.9) | collective-permute-done | bytes 163872 | tf_op jit(solution)/shard_map/ppermute | solution.py:28
  195.7 1.1 fusion.20
  197.3 1.2 fusion.25
  (315 shorter events, 65.2 us)
Async XLA Ops:
  0.9 11.6 %collective-permute-start = (bf16[16,4,256]{2,1,0:T(4,128)(2,1)S(1)}, bf16[16,4,256]{2,1,0:T(4,128)(2,1)S(1)}, u32[]{:S(2)}, u32[]{:S(2)}) collective-permute-start(bf16[16,4,256]{2,1,0:T(4,128)(2,1)S(1)} %get-tuple-element.140), channel_id=1, source_target_pairs={{0,16},{16,32},{32,48},{48,64},{64,80},{80,96},{96,112},{112,128},... | collective-permute-start | bytes 98312 | tf_op jit(solution)/shard_map/ppermute | solution.py:26
  8.4 9.5 %collective-permute-start.1 = (bf16[16,4,256]{2,1,0:T(4,128)(2,1)S(1)}, bf16[16,4,256]{2,1,0:T(4,128)(2,1)S(1)}, u32[]{:S(2)}, u32[]{:S(2)}) collective-permute-start(bf16[16,4,256]{2,1,0:T(4,128)(2,1)S(1)} %get-tuple-element.141), channel_id=1, source_target_pairs={{16,0},{32,16},{48,32},{64,48},{80,64},{96,80},{112,96},{128,112},... | collective-permute-start | bytes 98312 | tf_op jit(solution)/shard_map/ppermute | solution.py:28
  20.1 27.7 %all-to-all-start = ((bf16[16,16,8,256]{3,2,1,0:T(8,128)(2,1)}), bf16[16,16,8,256]{3,2,1,0:T(8,128)(2,1)S(1)}, u32[]{:S(2)}, u32[]{:S(2)}) async-start(bf16[16,16,8,256]{3,2,1,0:T(8,128)(2,1)} %stack.2), calls=%async_computation | async-start | bytes 2097152 | tf_op jit(solution)/shard_map/all_to_all | solution.py:119
  27.3 20.6 %copy-start = (s32[16]{0:T(128)S(1)}, s32[16]{0:T(128)}, u32[]{:S(2)}) copy-start(s32[16]{0:T(128)} %param.8) | copy-start | bytes 196
  138.9 7.3 %collective-permute-start.2 = (f32[4,1,4096]{2,1,0:T(1,128)S(1)}, f32[4,1,4096]{2,1,0:T(1,128)S(1)}, u32[]{:S(2)}, u32[]{:S(2)}) collective-permute-start(f32[4,1,4096]{2,1,0:T(1,128)S(1)} %get-tuple-element.138), channel_id=1, source_target_pairs={{0,16},{16,32},{32,48},{48,64},{64,80},{80,96},{96,112},{112,128},... | collective-permute-start | bytes 196616 | tf_op jit(solution)/shard_map/ppermute | solution.py:26
  144.3 9.8 %collective-permute-start.3 = (f32[4,1,4096]{2,1,0:T(1,128)S(1)}, f32[4,1,4096]{2,1,0:T(1,128)S(1)}, u32[]{:S(2)}, u32[]{:S(2)}) collective-permute-start(f32[4,1,4096]{2,1,0:T(1,128)S(1)} %get-tuple-element.139), channel_id=1, source_target_pairs={{16,0},{32,16},{48,32},{64,48},{80,64},{96,80},{112,96},{128,112},... | collective-permute-start | bytes 196616 | tf_op jit(solution)/shard_map/ppermute | solution.py:28
  154.2 7.1 %collective-permute-start.4 = (f32[1,10,4096]{2,1,0:T(8,128)S(1)}, f32[1,10,4096]{2,1,0:T(8,128)S(1)}, u32[]{:S(2)}, u32[]{:S(2)}) collective-permute-start(f32[1,10,4096]{2,1,0:T(8,128)S(1)} %get-tuple-element.136), channel_id=1, source_target_pairs={{0,1},{1,2},{2,3},{3,4},{4,5},{5,6},{6,7},{7,8},{8,9},{9,10},{10,1... | collective-permute-start | bytes 491528 | tf_op jit(solution)/shard_map/ppermute | solution.py:26
  156.9 9.2 %collective-permute-start.5 = (f32[1,10,4096]{2,1,0:T(8,128)S(1)}, f32[1,10,4096]{2,1,0:T(8,128)S(1)}, u32[]{:S(2)}, u32[]{:S(2)}) collective-permute-start(f32[1,10,4096]{2,1,0:T(8,128)S(1)} %get-tuple-element.137), channel_id=1, source_target_pairs={{1,0},{2,1},{3,2},{4,3},{5,4},{6,5},{7,6},{8,7},{9,8},{10,9},{11,1... | collective-permute-start | bytes 491528 | tf_op jit(solution)/shard_map/ppermute | solution.py:28
  169.7 5.3 %collective-permute-start.6 = (f32[4,1,4096]{2,1,0:T(1,128)S(1)}, f32[4,1,4096]{2,1,0:T(1,128)S(1)}, u32[]{:S(2)}, u32[]{:S(2)}) collective-permute-start(f32[4,1,4096]{2,1,0:T(1,128)S(1)} %get-tuple-element.132), channel_id=1, source_target_pairs={{0,16},{16,32},{32,48},{48,64},{64,80},{80,96},{96,112},{112,128},... | collective-permute-start | bytes 196616 | tf_op jit(solution)/shard_map/ppermute | solution.py:26
  173.0 9.8 %collective-permute-start.7 = (f32[4,1,4096]{2,1,0:T(1,128)S(1)}, f32[4,1,4096]{2,1,0:T(1,128)S(1)}, u32[]{:S(2)}, u32[]{:S(2)}) collective-permute-start(f32[4,1,4096]{2,1,0:T(1,128)S(1)} %get-tuple-element.133), channel_id=1, source_target_pairs={{16,0},{32,16},{48,32},{64,48},{80,64},{96,80},{112,96},{128,112},... | collective-permute-start | bytes 196616 | tf_op jit(solution)/shard_map/ppermute | solution.py:28
  182.9 7.1 %collective-permute-start.8 = (f32[1,10,4096]{2,1,0:T(8,128)S(1)}, f32[1,10,4096]{2,1,0:T(8,128)S(1)}, u32[]{:S(2)}, u32[]{:S(2)}) collective-permute-start(f32[1,10,4096]{2,1,0:T(8,128)S(1)} %get-tuple-element.134), channel_id=1, source_target_pairs={{0,1},{1,2},{2,3},{3,4},{4,5},{5,6},{6,7},{7,8},{8,9},{9,10},{10,1... | collective-permute-start | bytes 491528 | tf_op jit(solution)/shard_map/ppermute | solution.py:26
  185.3 9.2 %collective-permute-start.9 = (f32[1,10,4096]{2,1,0:T(8,128)S(1)}, f32[1,10,4096]{2,1,0:T(8,128)S(1)}, u32[]{:S(2)}, u32[]{:S(2)}) collective-permute-start(f32[1,10,4096]{2,1,0:T(8,128)S(1)} %get-tuple-element.135), channel_id=1, source_target_pairs={{1,0},{2,1},{3,2},{4,3},{5,4},{6,5},{7,6},{8,7},{9,8},{10,9},{11,1... | collective-permute-start | bytes 491528 | tf_op jit(solution)/shard_map/ppermute | solution.py:28
